TPU v7x, 32 devices: a whole 2x2x4 slice. The times are simulated.
32 devices in a mesh: group: 2 (over x), expert: 16 (over z, y, core).
Axes of the slice: x: 2, y: 2, z: 4, core: 2. Of those that a mesh axis runs over, the one named last changes fastest.
Arguments:
- tokens: bfloat16 [128, 7168], P(('group', 'expert')), parts along dimension 0, may hold values from -6 to 6
- expert_ids: int32 [128, 2], P(('group', 'expert')), parts along dimension 0, may hold values from 0 to 1, all different within a row; in each aligned block of 4 rows (0 to 3, 4 to 7, ...) at most 4 rows name the same one
- gate_codes: int32 [128, 2], P(('group', 'expert')), parts along dimension 0, may hold values from 1 to 65535
- gate_weight: bfloat16 [16, 7168, 256], P('expert'), may hold values from -0.0625 to 0.0625
- up_weight: bfloat16 [16, 7168, 256], P('expert'), may hold values from -0.0625 to 0.0625
- down_weight: bfloat16 [16, 256, 7168], P('expert'), may hold values from -0.125 to 0.125
- target_basis: bfloat16 [7168, 512], P('expert'), may hold values from -0.0625 to 0.0625
Outputs:
- targets: bfloat16 [128, 512], P(('group', 'expert')), parts along dimension 0
There are 2 independent parts, one for each index of `group`. A program takes and returns all parts, laid end to end along the dimension named above; an argument that names none is the same for every part. Nothing has to cross between parts.
Inputs may be any that keep to these rules, and one draw needn't show every extreme that they name: `expert_ids`: each row names 2 different experts; among the 4 rows of one device no expert is named more than 4 times, a bound that some block reaches.
All inputs are finite; a program needn't handle non-finite values.
Results may differ from a plain program's by a relative error of at most 0.0057.
Values may be sent and summed in bfloat16 or wider, within the bound.
No kernel may reach another device: no remote copies, remote signals or barrier semaphores. Data moves between devices by JAX's collectives and lax.ppermute only.
A program may use at most 128 MiB of HBM per device.

v0:
```python
import jax
import jax.numpy as jnp
from jax import lax
from jax.sharding import PartitionSpec as P

SLICES = 8


def run_expert(received, gate_weight, up_weight, down_weight):
    sources, slots, feature_width = received.shape
    row_block = received.reshape(sources * slots, feature_width)
    gate_act = jnp.dot(row_block, gate_weight[0], preferred_element_type=jnp.float32)
    up_act = jnp.dot(row_block, up_weight[0], preferred_element_type=jnp.float32)
    hidden = (jax.nn.silu(gate_act) * up_act).astype(jnp.bfloat16)
    expert_part = jnp.dot(hidden, down_weight[0], preferred_element_type=jnp.float32).astype(
        jnp.bfloat16
    )
    return expert_part.reshape(sources, slots, feature_width)


def shards(tokens, expert_ids, gate_codes, gate_weight, up_weight, down_weight, target_basis):
    token_count, feature_width = tokens.shape
    pick_count = expert_ids.shape[1]
    owner_count = lax.axis_size("expert")
    expert_count = owner_count // SLICES
    capacity = min(token_count, max(2, 5 * token_count * pick_count // (4 * expert_count)))
    rank_width = target_basis.shape[1]
    flat_ids = expert_ids.reshape(-1)
    onehot = (flat_ids[:, None] == jnp.arange(expert_count, dtype=jnp.int32)[None, :]).astype(
        jnp.int32
    )
    before = jnp.cumsum(onehot, axis=0) - onehot
    slot_rank = jnp.sum(before * onehot, axis=1)
    slot_index = flat_ids * capacity + slot_rank
    row_token = jnp.arange(token_count * pick_count, dtype=jnp.int32) // pick_count
    slot_table = (
        jnp.full((expert_count * capacity,), token_count, jnp.int32).at[slot_index].set(row_token)
    )
    padded = jnp.concatenate([tokens, jnp.zeros((1, feature_width), tokens.dtype)], axis=0)
    per_expert_rows = padded[slot_table].reshape(expert_count, 1, capacity, feature_width)
    outgoing = jnp.broadcast_to(per_expert_rows, (expert_count, SLICES, capacity, feature_width))
    outgoing = outgoing.reshape(owner_count, capacity, feature_width)
    full_basis = lax.all_gather(target_basis, "expert", axis=0, tiled=True)
    expert_part = run_expert(
        lax.all_to_all(outgoing, "expert", split_axis=0, concat_axis=0, tiled=True),
        gate_weight,
        up_weight,
        down_weight,
    )
    result = jnp.einsum("skd,dr->skr", expert_part, full_basis, preferred_element_type=jnp.float32)
    returned = lax.all_to_all(result, "expert", split_axis=0, concat_axis=0, tiled=True)
    summed = jnp.sum(returned.reshape(expert_count, SLICES, capacity, rank_width), axis=1)
    projected = summed.reshape(expert_count * capacity, rank_width)[slot_index]
    codes_float = gate_codes.astype(jnp.float32)
    weights = 2.5 * codes_float / jnp.sum(codes_float, axis=1, keepdims=True)
    projected = projected.reshape(token_count, pick_count, rank_width)
    return jnp.sum(weights[:, :, None] * projected, axis=1).astype(jnp.bfloat16)


def solution(mesh):
    in_specs = (
        P(("group", "expert"), None),
        P(("group", "expert"), None),
        P(("group", "expert"), None),
        P("expert", None, None),
        P("expert", None, None),
        P("expert", None, None),
        P("expert", None),
    )
    out_specs = P(("group", "expert"), None)
    return jax.shard_map(shards, mesh=mesh, in_specs=in_specs, out_specs=out_specs, check_vma=False)
```

profile of v0, /device:TPU:0, one launch (start us, length us, event | category | flops | bytes accessed | tf_op | source)
XLA Modules:
  0.0 121.8 jit_solution(8186890199680378276)
XLA Ops:
  6.5 0.7 all-gather.2.cloned.1.call-update
  7.3 0.8 copy.25
  8.1 0.7 broadcast_multiply_fusion
  8.8 0.1 copy.24
  8.9 0.1 mul.37
  9.0 0.2 reduce_window_sum.11
  9.2 0.8 concatenate.3
  10.1 0.6 scatter_custom_fusion
  10.7 0.6 gather_fusion
  11.4 1.2 broadcast_in_dim.8
  12.5 7.4 %all-to-all-start = ((bf16[16,4,7168]{2,1,0:T(4,128)(2,1)}), bf16[16,4,7168]{2,1,0:T(4,128)(2,1)S(1)}, u32[]{:S(2)}, u32[]{:S(2)}) async-start(bf16[16,4,7168]{2,1,0:T(4,128)(2,1)} %bitcast.2), calls=%async_computation | async-start | bytes 1835008 | tf_op jit(solution)/shard_map/all_to_all | solution.py:45
  20.0 35.1 %all-to-all-done = bf16[16,4,7168]{2,1,0:T(4,128)(2,1)S(1)} async-done(((bf16[16,4,7168]{2,1,0:T(4,128)(2,1)}), bf16[16,4,7168]{2,1,0:T(4,128)(2,1)S(1)}, u32[]{:S(2)}, u32[]{:S(2)}) %all-to-all-start) | async-done | bytes 917536 | tf_op jit(solution)/shard_map/all_to_all | solution.py:45
  55.1 0.2 reshape.53
  55.3 2.8 %fusion.5 = f32[64,256]{1,0:T(8,128)S(1)} fusion(bf16[64,7168]{1,0:T(8,128)(2,1)S(1)} %reshape.53, bf16[1,7168,256]{2,1,0:T(8,128)(2,1)} %param.10), kind=kOutput, calls=%fused_computation.9 | convolution fusion | flops 234881024 | bytes 4653056 | tf_op jit(solution)/shard_map/dot_general | solution.py:12
  58.0 5.5 %convolution_convert_fusion = bf16[64,7168]{1,0:T(8,128)(2,1)S(1)} fusion(bf16[1,256,7168]{2,1,0:T(8,128)(2,1)} %param.12, bf16[64,7168]{1,0:T(8,128)(2,1)S(1)} %reshape.53, bf16[1,7168,256]{2,1,0:T(8,128)(2,1)} %param.11, f32[64,256]{1,0:T(8,128)S(1)} %fusion.5), kind=kOutput, calls=%fused_computation.3 | convolution fusion | flops 470319104 | bytes 9240576 | tf_op jit(solution)/shard_map/dot_general | solution.py:15
  63.5 0.3 reshape.54
  63.8 33.4 %all-gather.2.cloned.1.call-done = bf16[7168,512]{1,0:T(8,128)(2,1)} async-done(((bf16[448,512]{1,0:T(8,128)(2,1)}), bf16[7168,512]{1,0:T(8,128)(2,1)}) %all-gather.2.cloned.1.call-update) | async-done | bytes 7340048 | tf_op jit(solution)/shard_map/all_gather | solution.py:43
  97.3 4.2 %fusion = f32[16,4,512]{2,0,1:T(8,128)S(1)} fusion(bf16[7168,512]{1,0:T(8,128)(2,1)} %all-gather.2.cloned.1.call-done, bf16[16,4,7168]{2,1,0:T(4,128)(2,1)S(1)} %reshape.54), kind=kOutput, calls=%fused_computation.4 | convolution fusion | flops 469762048 | bytes 8388608 | tf_op jit(solution)/shard_map/skd,dr->skr/dot_general | solution.py:50
  101.5 0.7 copy.27
  102.2 3.5 %all-to-all-start.1 = ((f32[16,4,512]{2,1,0:T(4,128)}), f32[16,4,512]{2,1,0:T(4,128)S(1)}, u32[]{:S(2)}, u32[]{:S(2)}) async-start(f32[16,4,512]{2,1,0:T(4,128)} %copy.27), calls=%async_computation.1 | async-start | bytes 262144 | tf_op jit(solution)/shard_map/all_to_all | solution.py:51
  105.8 0.1 copy.23
  105.9 7.8 %all-to-all-done.1 = f32[16,4,512]{2,1,0:T(4,128)S(1)} async-done(((f32[16,4,512]{2,1,0:T(4,128)}), f32[16,4,512]{2,1,0:T(4,128)S(1)}, u32[]{:S(2)}, u32[]{:S(2)}) %all-to-all-start.1) | async-done | bytes 131104 | tf_op jit(solution)/shard_map/all_to_all | solution.py:51
  113.7 0.6 gather_fusion.1
  114.2 0.7 multiply_reduce_fusion
  (17 shorter events, 0.3 us)
Async XLA Ops:
  6.5 13.4 %copy-start = (s32[4,2]{0,1:T(2,128)S(1)}, s32[4,2]{0,1:T(2,128)}, u32[]{:S(2)}) copy-start(s32[4,2]{0,1:T(2,128)} %param.9) | copy-start | bytes 100
  6.5 90.7 %all-gather.2.cloned.1.call-start = ((), (), s32[]{:S(2)}) async-start(), calls=%async_computation.2 | async-start | bytes 7798784 | tf_op jit(solution)/shard_map/all_gather | solution.py:43
  12.5 42.5 %all-to-all-start = ((bf16[16,4,7168]{2,1,0:T(4,128)(2,1)}), bf16[16,4,7168]{2,1,0:T(4,128)(2,1)S(1)}, u32[]{:S(2)}, u32[]{:S(2)}) async-start(bf16[16,4,7168]{2,1,0:T(4,128)(2,1)} %bitcast.2), calls=%async_computation | async-start | bytes 1835008 | tf_op jit(solution)/shard_map/all_to_all | solution.py:45
  102.2 11.4 %all-to-all-start.1 = ((f32[16,4,512]{2,1,0:T(4,128)}), f32[16,4,512]{2,1,0:T(4,128)S(1)}, u32[]{:S(2)}, u32[]{:S(2)}) async-start(f32[16,4,512]{2,1,0:T(4,128)} %copy.27), calls=%async_computation.1 | async-start | bytes 262144 | tf_op jit(solution)/shard_map/all_to_all | solution.py:51
Sparse Core Ops, SparseCore 0:
  9.6 87.5 all-gather.1
where the time goes:
time: 122 us
  waiting for transfers between devices  77 us (63%)
  between operations  13.5 us (11%)
  matrix products  12.4 us (10%)
  starting transfers between devices  10.9 us (9%)
  local copies, waits for them, and re-layouts  6.25 us (5%)
  other arithmetic  1.66 us (1%)
    all_to_all x1, waiting for transfers between devices, shards(): lax.all_to_all(outgoing, 'expert', split_axis=0, concat_axis=0, tiled=True)  35.1 us
    all_gather x1, waiting for transfers between devices, shards(): full_basis = lax.all_gather(target_basis, 'expert', axis=0, tiled=True)  33.4 us
    all_to_all x1, waiting for transfers between devices, shards(): lax.all_to_all(result, 'expert', split_axis=0, concat_axis=0, tiled=True)  7.76 us
    all_to_all x1, starting transfers between devices, shards(): lax.all_to_all(outgoing, 'expert', split_axis=0, concat_axis=0, tiled=True)  7.41 us
    dot_general x1, matrix products, run_expert(): jnp.dot(hidden, down_weight[0], preferred_element_type=jnp.float32)  5.45 us
    dot_general x1, matrix products, shards(): jnp.einsum('skd,dr->skr', expert_part, full_basis, preferred_element_type...  4.23 us
    all_to_all x1, starting transfers between devices, shards(): lax.all_to_all(result, 'expert', split_axis=0, concat_axis=0, tiled=True)  3.51 us
    dot_general x1, matrix products, run_expert(): jnp.dot(row_block, gate_weight[0], preferred_element_type=jnp.float32)  2.76 us
  transfers between devices with their start and end apart: 3, of which 3 were waited for; matrix products, arithmetic and copies ran while one was open for 12% of the time, Pallas kernels for 0%

commit v1 on v0

--- a/solution.py
+++ b/solution.py
@@ -1,9 +1,20 @@
+import functools
+
 import jax
 import jax.numpy as jnp
 from jax import lax
+from jax.experimental import pallas as pl
+from jax.experimental.pallas import tpu as pltpu
 from jax.sharding import PartitionSpec as P
 
+
 SLICES = 8
+CORES = 2
+COLUMNS = 2
+PLANES = 4
+FETCH_PARTS = 8
+LANES = 128
+MIB = 1 << 20
 
 
 def run_expert(received, gate_weight, up_weight, down_weight):
@@ -18,7 +29,9 @@
     return expert_part.reshape(sources, slots, feature_width)
 
 
-def shards(tokens, expert_ids, gate_codes, gate_weight, up_weight, down_weight, target_basis):
+def general_shards(
+    tokens, expert_ids, gate_codes, gate_weight, up_weight, down_weight, target_basis
+):
     token_count, feature_width = tokens.shape
     pick_count = expert_ids.shape[1]
     owner_count = lax.axis_size("expert")
@@ -57,6 +70,300 @@
     return jnp.sum(weights[:, :, None] * projected, axis=1).astype(jnp.bfloat16)
 
 
+def fetch_kernel(counts, index_ref, *refs):
+    del index_ref
+    sources, targets, sems = refs[: len(counts)], refs[len(counts) : -1], refs[-1]
+    copies = []
+    for source, target, count in zip(sources, targets, counts):
+        rows = target.shape[0] // count
+        for k in range(count):
+            block = pl.ds(k * rows, rows)
+            sem = sems.at[len(copies)]
+            copies.append(pltpu.make_async_copy(source.at[block, :], target.at[block, :], sem))
+            copies[-1].start()
+    for copy in copies:
+        copy.wait()
+
+
+def stack_blocks_kernel(*refs):
+    for n, block in enumerate(refs[:-1]):
+        refs[-1][n] = block[...]
+
+
+def stack_rows_kernel(sources, *refs):
+    out_ref = refs[-1]
+    for n, (ref, at) in enumerate(sources):
+        block = refs[ref][...] if at is None else refs[ref][at]
+        rows = block.shape[0]
+        out_ref[n * rows : (n + 1) * rows, :] = block
+
+
+def bits_of(index):
+    return tuple(jnp.bitwise_and(jnp.right_shift(index, n), 1) for n in range(4))
+
+
+def expert_kernel(index_ref, *refs):
+    places = CORES * COLUMNS
+    stacks = refs[:places]
+    gate_ref, up_ref, down_ref = refs[places : places + 3]
+    pieces, x_ref = refs[places + 3 : -1], refs[-1]
+    quarter, width = stacks[0].shape
+    half = COLUMNS * quarter
+    rows = quarter // PLANES
+    total = CORES * half
+    span = width // (COLUMNS * PLANES)
+    _, column, near, far = bits_of(index_ref[0])
+    for b, stack in enumerate(stacks):
+        x_ref[b * quarter : (b + 1) * quarter, :] = stack[...]
+    x = x_ref[...]
+    gate_act = jnp.dot(x, gate_ref[...], preferred_element_type=jnp.float32)
+    up_act = jnp.dot(x, up_ref[...], preferred_element_type=jnp.float32)
+    hidden = (gate_act / (1.0 + jnp.exp(-gate_act)) * up_act).astype(jnp.bfloat16)
+    to_row = lax.broadcasted_iota(jnp.int32, (total, total), 0)
+    from_row = lax.broadcasted_iota(jnp.int32, (total, total), 1)
+    wanted = jnp.bitwise_xor(from_row, column * quarter + (far * 2 + near) * rows)
+    order = jnp.where(to_row == wanted, 1.0, 0.0).astype(jnp.bfloat16)
+    hidden = jnp.dot(order, hidden, preferred_element_type=jnp.float32).astype(jnp.bfloat16)
+    for to_column in (1, 0):
+        for n, to_near in enumerate((1, 0)):
+            for to_far in (0, 1):
+                plane = to_far * 2 + jnp.bitwise_xor(near, to_near)
+                chip = plane * COLUMNS + jnp.bitwise_xor(column, to_column)
+                part = pl.ds(pl.multiple_of(chip * span, LANES), span)
+                out = jnp.dot(hidden, down_ref[:, part], preferred_element_type=jnp.float32)
+                out = out.astype(jnp.bfloat16)
+                for core in range(CORES):
+                    piece = pieces[core * COLUMNS + to_column]
+                    at = slice(to_far * span, (to_far + 1) * span)
+                    piece[n, :, at] = out[core * half : (core + 1) * half]
+
+
+def pick_kernel(index_ref, first, second, out_ref):
+    group = jnp.right_shift(index_ref[0], 4)
+    core = bits_of(index_ref[0])[0]
+
+    @pl.when(core == group)
+    def _():
+        out_ref[...] = first[...]
+
+    @pl.when(core != group)
+    def _():
+        out_ref[...] = second[...]
+
+
+def stack_kernel(index_ref, *refs):
+    core, _, _, far = bits_of(index_ref[0])
+    place = far * 2 + core
+    for b, shard in enumerate(refs[:-1]):
+        rows = shard.shape[0]
+        at = pl.multiple_of(jnp.bitwise_xor(place, b) * rows, rows)
+        refs[-1][pl.ds(at, rows), :] = shard[...]
+
+
+def part_total(at, own_ref, other_ref, crossed_ref):
+    total = own_ref[at].astype(jnp.float32) + other_ref[at].astype(jnp.float32)
+    return total + crossed_ref[0].astype(jnp.float32)
+
+
+def total_kernel(own_ref, other_ref, crossed_ref, out_ref):
+    out_ref[...] = part_total(0, own_ref, other_ref, crossed_ref).astype(out_ref.dtype)
+
+
+def basis_kernel(index_ref, own_ref, other_ref, crossed_ref, near_ref, basis_ref, *refs):
+    own_out, other_out, s_ref, o_ref = refs
+    half = near_ref.shape[0]
+    rows = half // (COLUMNS * PLANES)
+    _, column, near, far = bits_of(index_ref[0])
+    total = part_total(1, own_ref, other_ref, crossed_ref) + near_ref[...].astype(jnp.float32)
+    high = total.astype(jnp.bfloat16)
+    s_ref[:half, :] = high
+    s_ref[half:, :] = (total - high.astype(jnp.float32)).astype(jnp.bfloat16)
+    out = jnp.dot(s_ref[...], basis_ref[...], preferred_element_type=jnp.float32)
+    out = out[:half] + out[half:]
+    for p in range(COLUMNS * PLANES):
+        o_ref[p] = out[p * rows : (p + 1) * rows]
+    for n, step in enumerate((0, 2, 1, 3)):
+        plane = jnp.bitwise_xor(far * 2 + near, step)
+        own_out[n] = o_ref[column * PLANES + plane]
+        other_out[n] = o_ref[(1 - column) * PLANES + plane]
+
+
+def combine_kernel(index_ref, ids_ref, codes_ref, own_ref, far_ref, out_ref):
+    expert = bits_of(index_ref[0])[3]
+    codes = codes_ref[...].astype(jnp.float32)
+    gates = 2.5 * codes / jnp.sum(codes, axis=1, keepdims=True)
+    ids = ids_ref[...]
+    total = 0.0
+    for e, ref in ((expert, own_ref), (1 - expert, far_ref)):
+        gate = jnp.sum(jnp.where(ids == e, gates, 0.0), axis=1, keepdims=True)
+        total += gate * ref[0]
+    out_ref[...] = total.astype(out_ref.dtype)
+
+
+def sharded_basis_shards(
+    tokens, expert_ids, gate_codes, gate_weight, up_weight, down_weight, target_basis
+):
+    rows, width = tokens.shape
+    devices = lax.axis_size("expert")
+    place_count = CORES * COLUMNS
+    quarter = PLANES * rows
+    half = COLUMNS * quarter
+    span = 2 * width // (COLUMNS * PLANES)
+    shard, rank = target_basis.shape
+    index = lax.axis_index(("group", "expert")).astype(jnp.int32).reshape(1)
+    bf16 = jnp.bfloat16
+    vmem = pl.BlockSpec(memory_space=pltpu.VMEM)
+    smem = pl.BlockSpec(memory_space=pltpu.SMEM)
+    hbm = pl.BlockSpec(memory_space=pltpu.HBM)
+
+    def swap(x, step):
+        return lax.ppermute(x, "expert", [(i, i ^ step) for i in range(devices)])
+
+    def core_swap(x):
+        return swap(x, 1)
+
+    def column_swap(x):
+        return swap(x, CORES)
+
+    def plane_swap(x, step):
+        return swap(x, place_count * step)
+
+    def kernel(body, shapes, *operands, scratch=(), limit=4 * MIB, with_index=True):
+        operands = ((index,) if with_index else ()) + operands
+        specs = ([smem] if with_index else []) + [vmem] * (len(operands) - with_index)
+        return pl.pallas_call(
+            body,
+            out_shape=shapes,
+            in_specs=specs,
+            out_specs=jax.tree.map(lambda _: vmem, shapes),
+            scratch_shapes=scratch,
+            compiler_params=pltpu.CompilerParams(vmem_limit_bytes=limit),
+        )(*operands)
+
+    def shape(*dims, dtype=bf16):
+        return jax.ShapeDtypeStruct(dims, dtype)
+
+    def fetch(operands):
+        operands = [pltpu.with_memory_space_constraint(x, pltpu.HBM) for x in operands]
+        counts = [FETCH_PARTS if x.shape[0] % (16 * FETCH_PARTS) == 0 else 1 for x in operands]
+        out = pl.pallas_call(
+            functools.partial(fetch_kernel, counts),
+            out_shape=tuple(pltpu.VMEM(x.shape, x.dtype) for x in operands),
+            in_specs=[smem] + [hbm] * len(operands),
+            out_specs=(vmem,) * len(operands),
+            scratch_shapes=[pltpu.SemaphoreType.DMA((sum(counts),))],
+            compiler_params=pltpu.CompilerParams(vmem_limit_bytes=MIB),
+        )(index, *operands)
+        return [pltpu.with_memory_space_constraint(x, pltpu.VMEM) for x in out]
+
+    near = {d: plane_swap(tokens, d) for d in (2, 3, 1)}
+    own_far = column_swap(tokens)
+    gate, up, own = fetch((gate_weight[0], up_weight[0], tokens))
+    (down,) = fetch((down_weight[0],))
+    near = [near[d] for d in range(1, PLANES)]
+    relayed = kernel(stack_blocks_kernel, shape(PLANES - 1, rows, width), *near, with_index=False)
+    relayed = column_swap(relayed)
+    stacks = [
+        kernel(
+            functools.partial(stack_rows_kernel, [(d, None) for d in range(PLANES)]),
+            shape(quarter, width),
+            own,
+            *near,
+            with_index=False,
+        ),
+        kernel(
+            functools.partial(
+                stack_rows_kernel, [(0, None)] + [(1, d) for d in range(PLANES - 1)]
+            ),
+            shape(quarter, width),
+            own_far,
+            relayed,
+            with_index=False,
+        ),
+    ]
+    stacks += [core_swap(tokens_stack) for tokens_stack in stacks]
+
+    senders = [(g, i) for g in range(CORES) for i in range(devices) if i % CORES == g]
+    far_basis = lax.ppermute(
+        target_basis,
+        ("group", "expert"),
+        [(g * devices + i, g * devices + (i ^ 2 * place_count)) for g, i in senders],
+    )
+    group_basis = lax.ppermute(
+        far_basis,
+        ("group", "expert"),
+        [(g * devices + i, (1 - g) * devices + i) for g, i in senders],
+    )
+    far_basis = kernel(pick_kernel, shape(shard, rank), far_basis, group_basis)
+    basis = kernel(
+        stack_kernel,
+        shape(place_count * shard, rank),
+        target_basis,
+        core_swap(target_basis),
+        far_basis,
+        core_swap(far_basis),
+    )
+
+    piece = shape(2, half, span)
+    own_own, own_far, other_own, other_far = kernel(
+        expert_kernel,
+        (piece,) * place_count,
+        *stacks,
+        gate,
+        up,
+        down,
+        scratch=[pltpu.VMEM((place_count * quarter, width), bf16)],
+        limit=16 * MIB,
+    )
+
+    other_far = core_swap(other_far)
+    other_own = core_swap(other_own)
+    pairs = (own_far.astype(jnp.float32) + other_far.astype(jnp.float32)).astype(bf16)
+    first = column_swap(pairs[:1])
+    second = column_swap(pairs[1:])
+    total = kernel(total_kernel, shape(half, span), own_own, other_own, first, with_index=False)
+    out_piece = shape(PLANES, rows, rank, dtype=jnp.float32)
+    kept, sent = kernel(
+        basis_kernel,
+        (out_piece, out_piece),
+        own_own,
+        other_own,
+        second,
+        plane_swap(total, 1),
+        basis,
+        scratch=[
+            pltpu.VMEM((2 * half, span), bf16),
+            pltpu.VMEM((COLUMNS * PLANES, rows, rank), jnp.float32),
+        ],
+        limit=16 * MIB,
+    )
+    kept = kept + column_swap(sent)
+    kept = kept[:2] + plane_swap(kept[2:], 1)
+    return kernel(
+        combine_kernel, shape(rows, rank), expert_ids, gate_codes, kept[:1], plane_swap(kept[1:], 2)
+    )
+
+
+def fits(tokens, target_basis):
+    rows, width = tokens.shape
+    devices = lax.axis_size("expert")
+    return (
+        lax.axis_size("group") == CORES
+        and devices == CORES * COLUMNS * PLANES
+        and SLICES * 2 == devices
+        and rows & (rows - 1) == 0
+        and PLANES * rows % 16 == 0
+        and width % (COLUMNS * PLANES * LANES) == 0
+        and target_basis.shape[0] * devices == width
+        and target_basis.shape[0] % 16 == 0
+    )
+
+
+def shards(tokens, expert_ids, gate_codes, gate_weight, up_weight, down_weight, target_basis):
+    plan = sharded_basis_shards if fits(tokens, target_basis) else general_shards
+    return plan(tokens, expert_ids, gate_codes, gate_weight, up_weight, down_weight, target_basis)
+
+
 def solution(mesh):
     in_specs = (
         P(("group", "expert"), None),

time: 122 us -> 65.8 us (0.54)
  waiting for transfers between devices: 77 us -> 37.8 us
  between operations: 13.5 us -> 0.23 us
  matrix products: 12.4 us -> 0 us
  Pallas kernels: 0 us -> 9.02 us
  starting transfers between devices: 10.9 us -> 18.2 us
  local copies, waits for them, and re-layouts: 6.25 us -> 0.23 us
  other arithmetic: 1.66 us -> 0.07 us
    all_to_all x2 -> x0, waiting for transfers between devices: 42.8 us -> none  [the longest x1 35.1 us: shards(): lax.all_to_all(outgoing, 'expert', split_axis=0, concat_axis=0, tiled=True)]
    ppermute x0 -> x19, waiting for transfers between devices: none -> 37.8 us  [the longest x17 24.9 us: swap(): return lax.ppermute(x, 'expert', [(i, i ^ step) for i in range(devices)])]
    all_gather x1 -> x0, waiting for transfers between devices: 33.4 us -> none  [shards(): full_basis = lax.all_gather(target_basis, 'expert', axis=0, tiled=True)]
    ppermute x0 -> x19, starting transfers between devices: none -> 18.2 us  [the longest x17 13.8 us: swap(): return lax.ppermute(x, 'expert', [(i, i ^ step) for i in range(devices)])]
    dot_general x3 -> x0, matrix products: 12.4 us -> none  [the longest x1 5.45 us: run_expert(): jnp.dot(hidden, down_weight[0], preferred_element_type=jnp.float32)]
    all_to_all x2 -> x0, starting transfers between devices: 10.9 us -> none  [the longest x1 7.41 us: shards(): lax.all_to_all(outgoing, 'expert', split_axis=0, concat_axis=0, tiled=True)]
    pallas_call x0 -> x11, Pallas kernels: none -> 9.02 us  [the longest x2 5.33 us: fetch(): pl.pallas_call(functools.partial(fetch_kernel, counts), out_shape=tuple((...]
  transfers between devices with their start and end apart: 3 -> 19, of which waited for: 3 -> 11; matrix products, arithmetic and copies ran while one was open for 12% -> 0% of each run, Pallas kernels for 0% -> 12%
where the time goes in v1:
time: 65.8 us; the launch traced here: 65.6 us
  waiting for transfers between devices  37.8 us (57%)
  starting transfers between devices  18.2 us (28%)
  Pallas kernels  9.02 us (14%)
    ppermute x17, waiting for transfers between devices, swap(): return lax.ppermute(x, 'expert', [(i, i ^ step) for i in range(devices)])  24.9 us
    ppermute x17, starting transfers between devices, swap(): return lax.ppermute(x, 'expert', [(i, i ^ step) for i in range(devices)])  13.8 us
    ppermute x1, waiting for transfers between devices, sharded_basis_shards(): lax.ppermute(target_basis, ('group', 'expert'), [(g * devices + i, g * de...  7.04 us
    ppermute x1, waiting for transfers between devices, sharded_basis_shards(): lax.ppermute(far_basis, ('group', 'expert'), [(g * devices + i, (1 - g) *...  5.88 us
    pallas_call x2, Pallas kernels, fetch(): pl.pallas_call(functools.partial(fetch_kernel, counts), out_shape=tuple((...  5.33 us
    pallas_call x9, Pallas kernels, kernel(): pl.pallas_call(body, out_shape=shapes, in_specs=specs, out_specs=jax.tree...  3.69 us
    ppermute x1, starting transfers between devices, sharded_basis_shards(): lax.ppermute(target_basis, ('group', 'expert'), [(g * devices + i, g * de...  3.08 us
  transfers between devices with their start and end apart: 19, of which 11 were waited for; matrix products, arithmetic and copies ran while one was open for 0% of the time, Pallas kernels for 12%

profile of v1, /device:TPU:0, one launch (start us, length us, event | category | flops | bytes accessed | tf_op | source)
XLA Modules:
  0.0 65.6 jit_solution(1016783796447220795)
XLA Ops:
  0.0 3.1 %collective-permute-start = (bf16[4,7168]{1,0:T(4,128)(2,1)}, bf16[4,7168]{1,0:T(4,128)(2,1)S(1)}, u32[]{:S(2)}, u32[]{:S(2)}) collective-permute-start(bf16[4,7168]{1,0:T(4,128)(2,1)} %refs_2_.1), channel_id=1, source_target_pairs={{0,4},{1,5},{2,6},{3,7},{4,0},{5,1},{6,2},{7,3},{8,12},{9,13},{10,... | collective-permute-start | bytes 172040 | tf_op jit(solution)/shard_map/ppermute | solution.py:220
  3.1 2.6 %collective-permute-start.1 = (bf16[4,7168]{1,0:T(4,128)(2,1)}, bf16[4,7168]{1,0:T(4,128)(2,1)S(1)}, u32[]{:S(2)}, u32[]{:S(2)}) collective-permute-start(bf16[4,7168]{1,0:T(4,128)(2,1)} %refs_2_.1), channel_id=1, source_target_pairs={{0,8},{1,9},{2,10},{3,11},{4,12},{5,13},{6,14},{7,15},{8,0},{9,1},... | collective-permute-start | bytes 172040 | tf_op jit(solution)/shard_map/ppermute | solution.py:220
  5.6 3.8 %collective-permute-done.1.refs_2_.refs_1_ = bf16[4,7168]{1,0:T(4,128)(2,1)S(1)} collective-permute-done((bf16[4,7168]{1,0:T(4,128)(2,1)}, bf16[4,7168]{1,0:T(4,128)(2,1)S(1)}, u32[]{:S(2)}, u32[]{:S(2)}) %collective-permute-start.1) | collective-permute-done | bytes 57376 | tf_op jit(solution)/shard_map/ppermute | solution.py:220
  9.5 2.4 %collective-permute-done.2.refs_3_.refs_2_ = bf16[4,7168]{1,0:T(4,128)(2,1)S(1)} collective-permute-done((bf16[4,7168]{1,0:T(4,128)(2,1)}, bf16[4,7168]{1,0:T(4,128)(2,1)S(1)}, u32[]{:S(2)}, u32[]{:S(2)}) %collective-permute-start.2) | collective-permute-done | bytes 57376 | tf_op jit(solution)/shard_map/ppermute | solution.py:220
  11.8 1.6 %collective-permute-start.4 = (bf16[3,4,7168]{2,1,0:T(4,128)(2,1)S(1)}, bf16[3,4,7168]{2,1,0:T(4,128)(2,1)S(1)}, u32[]{:S(2)}, u32[]{:S(2)}) collective-permute-start(bf16[3,4,7168]{2,1,0:T(4,128)(2,1)S(1)} %shard_map.75), channel_id=1, source_target_pairs={{0,2},{1,3},{2,0},{3,1},{4,6},{5,7},{6,4},{7,5},{8,10},{9,11},{10,... | collective-permute-start | bytes 516104 | tf_op jit(solution)/shard_map/ppermute | solution.py:220
  13.4 0.5 collective-permute-start.3
  13.9 3.3 %shard_map.73 = (bf16[7168,256]{1,0:T(8,128)(2,1)S(1)}, bf16[7168,256]{1,0:T(8,128)(2,1)S(1)}, bf16[4,7168]{1,0:T(4,128)(2,1)S(1)}) custom-call(s32[1]{0:T(128)} %bitcast.index_ref, bf16[7168,256]{1,0:T(8,128)(2,1)} %bitcast.4, bf16[7168,256]{1,0:T(8,128)(2,1)} %bitcast.5, bf16[4,7168]{1,0:T(4,128)(2,1)} %refs_2_.1), custom_call_target="tpu_custom_call" | custom-call | tf_op jit(solution)/shard_map/pallas_call | solution.py:249
  17.4 0.6 collective-permute-done.3.refs_0_
  18.1 3.1 %collective-permute-start.13 = (bf16[448,512]{1,0:T(8,128)(2,1)S(1)}, bf16[448,512]{1,0:T(8,128)(2,1)S(1)}, u32[]{:S(2)}, u32[]{:S(2)}) collective-permute-start(bf16[448,512]{1,0:T(8,128)(2,1)S(1)} %copy-done), channel_id=1, source_target_pairs={{0,8},{2,10},{4,12},{6,14},{8,0},{10,2},{12,4},{14,6},{17,25},{19,... | collective-permute-start | bytes 1376264 | tf_op jit(solution)/shard_map/ppermute | solution.py:287
  21.2 2.1 %shard_map.77.refs_6_ = bf16[256,7168]{1,0:T(8,128)(2,1)S(1)} custom-call(s32[1]{0:T(128)} %bitcast.index_ref, bf16[256,7168]{1,0:T(8,128)(2,1)} %bitcast.6), custom_call_target="tpu_custom_call" | custom-call | tf_op jit(solution)/shard_map/pallas_call | solution.py:249
  23.3 2.2 %shard_map.78 = (bf16[2,32,1792]{2,1,0:T(8,128)(2,1)S(1)}, bf16[2,32,1792]{2,1,0:T(8,128)(2,1)S(1)}, bf16[2,32,1792]{2,1,0:T(8,128)(2,1)S(1)}, bf16[2,32,1792]{2,1,0:T(8,128)(2,1)S(1)}) custom-call(s32[1]{0:T(128)} %bitcast.index_ref, bf16[16,7168]{1,0:T(8,128)(2,1)S(1)} %shard_map.74.refs_0_, bf16[16,7168]{1,0:T(8,128)(2,1)S(1)} %shard_map.76.refs_1_, ...), custom_call_target="tpu_custom_call" | custom-call | tf_op jit(solution)/shard_map/pallas_call | solution.py:234
  26.1 7.0 %collective-permute-done.13.first = bf16[448,512]{1,0:T(8,128)(2,1)S(1)} collective-permute-done((bf16[448,512]{1,0:T(8,128)(2,1)S(1)}, bf16[448,512]{1,0:T(8,128)(2,1)S(1)}, u32[]{:S(2)}, u32[]{:S(2)}) %collective-permute-start.13) | collective-permute-done | bytes 458784 | tf_op jit(solution)/shard_map/ppermute | solution.py:287
  33.1 1.3 %collective-permute-start.14 = (bf16[448,512]{1,0:T(8,128)(2,1)S(1)}, bf16[448,512]{1,0:T(8,128)(2,1)S(1)}, u32[]{:S(2)}, u32[]{:S(2)}) collective-permute-start(bf16[448,512]{1,0:T(8,128)(2,1)S(1)} %collective-permute-done.13.first), channel_id=1, source_target_pairs={{0,16},{2,18},{4,20},{6,22},{8,24},{10,26},{12,28},{14,30},{17,1},... | collective-permute-start | bytes 1376264 | tf_op jit(solution)/shard_map/ppermute | solution.py:292
  34.5 5.9 %collective-permute-done.14.second = bf16[448,512]{1,0:T(8,128)(2,1)S(1)} collective-permute-done((bf16[448,512]{1,0:T(8,128)(2,1)S(1)}, bf16[448,512]{1,0:T(8,128)(2,1)S(1)}, u32[]{:S(2)}, u32[]{:S(2)}) %collective-permute-start.14) | collective-permute-done | bytes 458784 | tf_op jit(solution)/shard_map/ppermute | solution.py:292
  40.9 1.6 %collective-permute-start.10 = (bf16[1,32,1792]{2,1,0:T(8,128)(2,1)S(1)}, bf16[1,32,1792]{2,1,0:T(8,128)(2,1)S(1)}, u32[]{:S(2)}, u32[]{:S(2)}) collective-permute-start(bf16[1,32,1792]{2,1,0:T(8,128)(2,1)S(1)} %get-tuple-element.23), channel_id=1, source_target_pairs={{0,2},{1,3},{2,0},{3,1},{4,6},{5,7},{6,4},{7,5},{8,10},{9,11},{10,... | collective-permute-start | bytes 344072 | tf_op jit(solution)/shard_map/ppermute | solution.py:220
  43.0 4.0 %collective-permute-done.10.crossed_ref = bf16[1,32,1792]{2,1,0:T(8,128)(2,1)S(1)} collective-permute-done((bf16[1,32,1792]{2,1,0:T(8,128)(2,1)S(1)}, bf16[1,32,1792]{2,1,0:T(8,128)(2,1)S(1)}, u32[]{:S(2)}, u32[]{:S(2)}) %collective-permute-start.10) | collective-permute-done | bytes 114720 | tf_op jit(solution)/shard_map/ppermute | solution.py:220
  47.3 1.3 %collective-permute-done.9.crossed_ref = bf16[1,32,1792]{2,1,0:T(8,128)(2,1)S(1)} collective-permute-done((bf16[1,32,1792]{2,1,0:T(8,128)(2,1)S(1)}, bf16[1,32,1792]{2,1,0:T(8,128)(2,1)S(1)}, u32[]{:S(2)}, u32[]{:S(2)}) %collective-permute-start.9) | collective-permute-done | bytes 114720 | tf_op jit(solution)/shard_map/ppermute | solution.py:220
  48.6 3.3 %collective-permute-done.11.near_ref = bf16[32,1792]{1,0:T(8,128)(2,1)S(1)} collective-permute-done((bf16[32,1792]{1,0:T(8,128)(2,1)S(1)}, bf16[32,1792]{1,0:T(8,128)(2,1)S(1)}, u32[]{:S(2)}, u32[]{:S(2)}) %collective-permute-start.11) | collective-permute-done | bytes 114720 | tf_op jit(solution)/shard_map/ppermute | solution.py:220
  52.4 1.6 %collective-permute-start.16 = (f32[4,4,512]{2,1,0:T(4,128)S(1)}, f32[4,4,512]{2,1,0:T(4,128)S(1)}, u32[]{:S(2)}, u32[]{:S(2)}) collective-permute-start(f32[4,4,512]{2,1,0:T(4,128)S(1)} %get-tuple-element.22), channel_id=1, source_target_pairs={{0,2},{1,3},{2,0},{3,1},{4,6},{5,7},{6,4},{7,5},{8,10},{9,11},{10,... | collective-permute-start | bytes 98312 | tf_op jit(solution)/shard_map/ppermute | solution.py:220
  54.0 2.4 %collective-permute-done.16 = f32[4,4,512]{2,1,0:T(4,128)S(1)} collective-permute-done((f32[4,4,512]{2,1,0:T(4,128)S(1)}, f32[4,4,512]{2,1,0:T(4,128)S(1)}, u32[]{:S(2)}, u32[]{:S(2)}) %collective-permute-start.16) | collective-permute-done | bytes 32800 | tf_op jit(solution)/shard_map/ppermute | solution.py:220
  56.5 3.7 %collective-permute-done.17 = f32[2,4,512]{2,1,0:T(4,128)S(1)} collective-permute-done((f32[2,4,512]{2,1,0:T(4,128)S(1)}, f32[2,4,512]{2,1,0:T(4,128)S(1)}, u32[]{:S(2)}, u32[]{:S(2)}) %collective-permute-start.17) | collective-permute-done | bytes 16416 | tf_op jit(solution)/shard_map/ppermute | solution.py:220
  60.2 1.0 %collective-permute-start.18 = (f32[1,4,512]{2,1,0:T(4,128)S(1)}, f32[1,4,512]{2,1,0:T(4,128)S(1)}, u32[]{:S(2)}, u32[]{:S(2)}) collective-permute-start(f32[1,4,512]{2,1,0:T(4,128)S(1)} %get-tuple-element.25), channel_id=1, source_target_pairs={{0,8},{1,9},{2,10},{3,11},{4,12},{5,13},{6,14},{7,15},{8,0},{9,1},... | collective-permute-start | bytes 24584 | tf_op jit(solution)/shard_map/ppermute | solution.py:220
  61.4 3.4 %collective-permute-done.18.far_ref = f32[1,4,512]{2,1,0:T(4,128)S(1)} collective-permute-done((f32[1,4,512]{2,1,0:T(4,128)S(1)}, f32[1,4,512]{2,1,0:T(4,128)S(1)}, u32[]{:S(2)}, u32[]{:S(2)}) %collective-permute-start.18) | collective-permute-done | bytes 8224 | tf_op jit(solution)/shard_map/ppermute | solution.py:220
  64.8 0.8 %shard_map.83 = bf16[4,512]{1,0:T(4,128)(2,1)} custom-call(s32[1]{0:T(128)} %bitcast.index_ref, s32[4,2]{1,0:T(4,128)S(1)} %copy.8.ids_ref, s32[4,2]{1,0:T(4,128)S(1)} %copy.9.codes_ref, f32[1,4,512]{2,1,0:T(4,128)S(1)} %get-tuple-element.26.own_ref, f32[1,4,512]{2,1,0:T(4,128)S(1)} %collective-permute-done.18.far_ref), custom_call_target="tpu_custom_call" | custom-call | tf_op jit(solution)/shard_map/pallas_call | solution.py:234
  (39 shorter events, 3.0 us)
Async XLA Ops:
  0.0 5.6 %collective-permute-start = (bf16[4,7168]{1,0:T(4,128)(2,1)}, bf16[4,7168]{1,0:T(4,128)(2,1)S(1)}, u32[]{:S(2)}, u32[]{:S(2)}) collective-permute-start(bf16[4,7168]{1,0:T(4,128)(2,1)} %refs_2_.1), channel_id=1, source_target_pairs={{0,4},{1,5},{2,6},{3,7},{4,0},{5,1},{6,2},{7,3},{8,12},{9,13},{10,... | collective-permute-start | bytes 172040 | tf_op jit(solution)/shard_map/ppermute | solution.py:220
  3.1 6.4 %collective-permute-start.1 = (bf16[4,7168]{1,0:T(4,128)(2,1)}, bf16[4,7168]{1,0:T(4,128)(2,1)S(1)}, u32[]{:S(2)}, u32[]{:S(2)}) collective-permute-start(bf16[4,7168]{1,0:T(4,128)(2,1)} %refs_2_.1), channel_id=1, source_target_pairs={{0,8},{1,9},{2,10},{3,11},{4,12},{5,13},{6,14},{7,15},{8,0},{9,1},... | collective-permute-start | bytes 172040 | tf_op jit(solution)/shard_map/ppermute | solution.py:220
  5.6 6.2 %collective-permute-start.2 = (bf16[4,7168]{1,0:T(4,128)(2,1)}, bf16[4,7168]{1,0:T(4,128)(2,1)S(1)}, u32[]{:S(2)}, u32[]{:S(2)}) collective-permute-start(bf16[4,7168]{1,0:T(4,128)(2,1)} %refs_2_.1), channel_id=1, source_target_pairs={{0,12},{1,13},{2,14},{3,15},{4,8},{5,9},{6,10},{7,11},{8,4},{9,5},... | collective-permute-start | bytes 172040 | tf_op jit(solution)/shard_map/ppermute | solution.py:220
  11.8 6.1 %collective-permute-start.4 = (bf16[3,4,7168]{2,1,0:T(4,128)(2,1)S(1)}, bf16[3,4,7168]{2,1,0:T(4,128)(2,1)S(1)}, u32[]{:S(2)}, u32[]{:S(2)}) collective-permute-start(bf16[3,4,7168]{2,1,0:T(4,128)(2,1)S(1)} %shard_map.75), channel_id=1, source_target_pairs={{0,2},{1,3},{2,0},{3,1},{4,6},{5,7},{6,4},{7,5},{8,10},{9,11},{10,... | collective-permute-start | bytes 516104 | tf_op jit(solution)/shard_map/ppermute | solution.py:220
  13.4 4.5 %collective-permute-start.3 = (bf16[4,7168]{1,0:T(4,128)(2,1)}, bf16[4,7168]{1,0:T(4,128)(2,1)S(1)}, u32[]{:S(2)}, u32[]{:S(2)}) collective-permute-start(bf16[4,7168]{1,0:T(4,128)(2,1)} %refs_2_.1), channel_id=1, source_target_pairs={{0,2},{1,3},{2,0},{3,1},{4,6},{5,7},{6,4},{7,5},{8,10},{9,11},{10,... | collective-permute-start | bytes 172040 | tf_op jit(solution)/shard_map/ppermute | solution.py:220
  13.9 4.1 %copy-start = (bf16[448,512]{1,0:T(8,128)(2,1)S(1)}, bf16[448,512]{1,0:T(8,128)(2,1)}, u32[]{:S(2)}) copy-start(bf16[448,512]{1,0:T(8,128)(2,1)} %refs_0_.1) | copy-start | bytes 1376260
  17.3 6.0 %collective-permute-start.5 = (bf16[16,7168]{1,0:T(8,128)(2,1)S(1)}, bf16[16,7168]{1,0:T(8,128)(2,1)S(1)}, u32[]{:S(2)}, u32[]{:S(2)}) collective-permute-start(bf16[16,7168]{1,0:T(8,128)(2,1)S(1)} %shard_map.74.refs_0_), channel_id=1, source_target_pairs={{0,1},{1,0},{2,3},{3,2},{4,5},{5,4},{6,7},{7,6},{8,9},{9,8},{10,11... | collective-permute-start | bytes 688136 | tf_op jit(solution)/shard_map/ppermute | solution.py:220
  18.0 5.3 %collective-permute-start.6 = (bf16[16,7168]{1,0:T(8,128)(2,1)S(1)}, bf16[16,7168]{1,0:T(8,128)(2,1)S(1)}, u32[]{:S(2)}, u32[]{:S(2)}) collective-permute-start(bf16[16,7168]{1,0:T(8,128)(2,1)S(1)} %shard_map.76.refs_1_), channel_id=1, source_target_pairs={{0,1},{1,0},{2,3},{3,2},{4,5},{5,4},{6,7},{7,6},{8,9},{9,8},{10,11... | collective-permute-start | bytes 688136 | tf_op jit(solution)/shard_map/ppermute | solution.py:220
  18.1 15.0 %collective-permute-start.13 = (bf16[448,512]{1,0:T(8,128)(2,1)S(1)}, bf16[448,512]{1,0:T(8,128)(2,1)S(1)}, u32[]{:S(2)}, u32[]{:S(2)}) collective-permute-start(bf16[448,512]{1,0:T(8,128)(2,1)S(1)} %copy-done), channel_id=1, source_target_pairs={{0,8},{2,10},{4,12},{6,14},{8,0},{10,2},{12,4},{14,6},{17,25},{19,... | collective-permute-start | bytes 1376264 | tf_op jit(solution)/shard_map/ppermute | solution.py:287
  25.4 9.0 %collective-permute-start.8 = (bf16[2,32,1792]{2,1,0:T(8,128)(2,1)S(1)}, bf16[2,32,1792]{2,1,0:T(8,128)(2,1)S(1)}, u32[]{:S(2)}, u32[]{:S(2)}) collective-permute-start(bf16[2,32,1792]{2,1,0:T(8,128)(2,1)S(1)} %get-tuple-element.20), channel_id=1, source_target_pairs={{0,1},{1,0},{2,3},{3,2},{4,5},{5,4},{6,7},{7,6},{8,9},{9,8},{10,11... | collective-permute-start | bytes 688136 | tf_op jit(solution)/shard_map/ppermute | solution.py:220
  25.5 21.6 %collective-permute-start.12 = (bf16[448,512]{1,0:T(8,128)(2,1)S(1)}, bf16[448,512]{1,0:T(8,128)(2,1)S(1)}, u32[]{:S(2)}, u32[]{:S(2)}) collective-permute-start(bf16[448,512]{1,0:T(8,128)(2,1)S(1)} %copy-done), channel_id=1, source_target_pairs={{0,1},{1,0},{2,3},{3,2},{4,5},{5,4},{6,7},{7,6},{8,9},{9,8},{10,11... | collective-permute-start | bytes 1376264 | tf_op jit(solution)/shard_map/ppermute | solution.py:220
  26.0 17.0 %collective-permute-start.7 = (bf16[2,32,1792]{2,1,0:T(8,128)(2,1)S(1)}, bf16[2,32,1792]{2,1,0:T(8,128)(2,1)S(1)}, u32[]{:S(2)}, u32[]{:S(2)}) collective-permute-start(bf16[2,32,1792]{2,1,0:T(8,128)(2,1)S(1)} %get-tuple-element.18), channel_id=1, source_target_pairs={{0,1},{1,0},{2,3},{3,2},{4,5},{5,4},{6,7},{7,6},{8,9},{9,8},{10,11... | collective-permute-start | bytes 688136 | tf_op jit(solution)/shard_map/ppermute | solution.py:220
  33.1 7.3 %collective-permute-start.14 = (bf16[448,512]{1,0:T(8,128)(2,1)S(1)}, bf16[448,512]{1,0:T(8,128)(2,1)S(1)}, u32[]{:S(2)}, u32[]{:S(2)}) collective-permute-start(bf16[448,512]{1,0:T(8,128)(2,1)S(1)} %collective-permute-done.13.first), channel_id=1, source_target_pairs={{0,16},{2,18},{4,20},{6,22},{8,24},{10,26},{12,28},{14,30},{17,1},... | collective-permute-start | bytes 1376264 | tf_op jit(solution)/shard_map/ppermute | solution.py:292
  40.4 20.8 %copy-start.1 = (s32[4,2]{0,1:T(2,128)S(1)}, s32[4,2]{0,1:T(2,128)}, u32[]{:S(2)}) copy-start(s32[4,2]{0,1:T(2,128)} %param.8) | copy-start | bytes 100
  40.4 20.9 %copy-start.2 = (s32[4,2]{0,1:T(2,128)S(1)}, s32[4,2]{0,1:T(2,128)}, u32[]{:S(2)}) copy-start(s32[4,2]{0,1:T(2,128)} %param.9) | copy-start | bytes 100
  40.5 6.7 %collective-permute-start.15 = (bf16[448,512]{1,0:T(8,128)(2,1)S(1)}, bf16[448,512]{1,0:T(8,128)(2,1)S(1)}, u32[]{:S(2)}, u32[]{:S(2)}) collective-permute-start(bf16[448,512]{1,0:T(8,128)(2,1)S(1)} %shard_map.80.refs_2_), channel_id=1, source_target_pairs={{0,1},{1,0},{2,3},{3,2},{4,5},{5,4},{6,7},{7,6},{8,9},{9,8},{10,11... | collective-permute-start | bytes 1376264 | tf_op jit(solution)/shard_map/ppermute | solution.py:220
  40.9 6.1 %collective-permute-start.10 = (bf16[1,32,1792]{2,1,0:T(8,128)(2,1)S(1)}, bf16[1,32,1792]{2,1,0:T(8,128)(2,1)S(1)}, u32[]{:S(2)}, u32[]{:S(2)}) collective-permute-start(bf16[1,32,1792]{2,1,0:T(8,128)(2,1)S(1)} %get-tuple-element.23), channel_id=1, source_target_pairs={{0,2},{1,3},{2,0},{3,1},{4,6},{5,7},{6,4},{7,5},{8,10},{9,11},{10,... | collective-permute-start | bytes 344072 | tf_op jit(solution)/shard_map/ppermute | solution.py:220
  42.5 6.1 %collective-permute-start.9 = (bf16[1,32,1792]{2,1,0:T(8,128)(2,1)S(1)}, bf16[1,32,1792]{2,1,0:T(8,128)(2,1)S(1)}, u32[]{:S(2)}, u32[]{:S(2)}) collective-permute-start(bf16[1,32,1792]{2,1,0:T(8,128)(2,1)S(1)} %get-tuple-element.24), channel_id=1, source_target_pairs={{0,2},{1,3},{2,0},{3,1},{4,6},{5,7},{6,4},{7,5},{8,10},{9,11},{10,... | collective-permute-start | bytes 344072 | tf_op jit(solution)/shard_map/ppermute | solution.py:220
  47.1 4.9 %collective-permute-start.11 = (bf16[32,1792]{1,0:T(8,128)(2,1)S(1)}, bf16[32,1792]{1,0:T(8,128)(2,1)S(1)}, u32[]{:S(2)}, u32[]{:S(2)}) collective-permute-start(bf16[32,1792]{1,0:T(8,128)(2,1)S(1)} %shard_map.79), channel_id=1, source_target_pairs={{0,4},{1,5},{2,6},{3,7},{4,0},{5,1},{6,2},{7,3},{8,12},{9,13},{10,... | collective-permute-start | bytes 344072 | tf_op jit(solution)/shard_map/ppermute | solution.py:220
  52.4 4.0 %collective-permute-start.16 = (f32[4,4,512]{2,1,0:T(4,128)S(1)}, f32[4,4,512]{2,1,0:T(4,128)S(1)}, u32[]{:S(2)}, u32[]{:S(2)}) collective-permute-start(f32[4,4,512]{2,1,0:T(4,128)S(1)} %get-tuple-element.22), channel_id=1, source_target_pairs={{0,2},{1,3},{2,0},{3,1},{4,6},{5,7},{6,4},{7,5},{8,10},{9,11},{10,... | collective-permute-start | bytes 98312 | tf_op jit(solution)/shard_map/ppermute | solution.py:220
  56.4 3.8 %collective-permute-start.17 = (f32[2,4,512]{2,1,0:T(4,128)S(1)}, f32[2,4,512]{2,1,0:T(4,128)S(1)}, u32[]{:S(2)}, u32[]{:S(2)}) collective-permute-start(f32[2,4,512]{2,1,0:T(4,128)S(1)} %slice.27), channel_id=1, source_target_pairs={{0,4},{1,5},{2,6},{3,7},{4,0},{5,1},{6,2},{7,3},{8,12},{9,13},{10,... | collective-permute-start | bytes 49160 | tf_op jit(solution)/shard_map/ppermute | solution.py:220
  60.2 4.6 %collective-permute-start.18 = (f32[1,4,512]{2,1,0:T(4,128)S(1)}, f32[1,4,512]{2,1,0:T(4,128)S(1)}, u32[]{:S(2)}, u32[]{:S(2)}) collective-permute-start(f32[1,4,512]{2,1,0:T(4,128)S(1)} %get-tuple-element.25), channel_id=1, source_target_pairs={{0,8},{1,9},{2,10},{3,11},{4,12},{5,13},{6,14},{7,15},{8,0},{9,1},... | collective-permute-start | bytes 24584 | tf_op jit(solution)/shard_map/ppermute | solution.py:220
